TPU v7x, 32 devices: a whole 2x2x4 slice. The times are simulated.
32 devices in a mesh: grp: 2 (over core), brick: 16 (over z, y, x).
Axes of the slice: x: 2, y: 2, z: 4, core: 2. Of those that a mesh axis runs over, the one named last changes fastest.
Arguments:
- density: float32 [64, 64, 256], P('brick', None, 'grp'), may hold values from 0.5 to 2
- energy_field: float32 [64, 64, 256], P('brick', None, 'grp'), may hold values from -6 to 6
- lepton_field: float32 [64, 64, 256], P('brick', None, 'grp'), may hold values from 0.1 to 0.6
- velocity: float32 [3, 64, 64, 256], P(None, 'brick', None, 'grp'), may hold values from -4 to 4
- abundance: float32 [2, 16, 1024, 128], P('grp', 'brick'), may hold values from -1.2 to 1.2
- tracer_mass: float32 [2, 16, 1024], P('grp', 'brick'), may hold values from 0.2 to 1
- tracer_cell: int32 [2, 16, 1024], P('grp', 'brick'), may hold values from 0 to 32767
- tracer_count: int32 [2, 16], P('grp', 'brick'), may hold values from 1 to 1024, as said below
- weak_rates: float32 [128, 128], replicated, may hold values from -0.5 to 0.5
- capture_rates: float32 [128, 128], replicated, may hold values from -0.5 to 0.5
- binding: float32 [128], replicated, may hold values from -6 to 6
- charge_ratio: float32 [128], replicated, may hold values from 0 to 1
Outputs:
- density_out: float32 [64, 64, 256], P('brick', None, 'grp')
- energy_out: float32 [64, 64, 256], P('brick', None, 'grp')
- lepton_out: float32 [64, 64, 256], P('brick', None, 'grp')
- abundance_out: float32 [2, 16, 1024, 128], P('grp', 'brick')
Inputs may be any that keep to these rules, and one draw needn't show every extreme that they name: `tracer_count`: for each index of grp the counts sum to 8192; exactly one brick of each half holds 1024, the most; every other brick holds at most 512, and some brick of each half holds exactly 512.
All inputs are finite; a program needn't handle non-finite values.
Results may differ from a plain program's by a relative error of at most 0.00029.
Values sent between devices are 32-bit elements; how exact they have to be, the bound alone decides.
A program may use at most 64 MiB of HBM per device.

v0:
```python
import functools

import jax
import jax.numpy as jnp
from jax import lax
from jax.experimental import pallas as pl
from jax.experimental.pallas import tpu as pltpu
from jax.sharding import PartitionSpec as P

NEWTON = 2
SWEEPS = 8
courant = 0.8
f32 = jnp.float32
bf16 = jnp.bfloat16
BLOCK = 256
MESH = pl.DeviceIdType.MESH


def split(values):
    high = values.astype(bf16)
    low = (values - high.astype(f32)).astype(bf16)
    return high, low


def dot(a, b, dims=((1,), (0,))):
    return lax.dot_general(a, b, (dims, ((), ())), preferred_element_type=f32)


def five_point(lower2, lower1, upper1, upper2):
    return 8.0 * (upper1 - lower1) - (upper2 - lower2)


def y_part(g):
    n = g.shape[0]
    return five_point(
        pltpu.roll(g, 2, 0), pltpu.roll(g, 1, 0), pltpu.roll(g, n - 1, 0), pltpu.roll(g, n - 2, 0)
    )


def z_part(h, other):
    n = h.shape[1]
    lane = lax.broadcasted_iota(jnp.int32, h.shape, 1)
    return five_point(
        pltpu.roll(jnp.where(lane >= n - 2, other, h), 2, 1),
        pltpu.roll(jnp.where(lane >= n - 1, other, h), 1, 1),
        pltpu.roll(jnp.where(lane < 1, other, h), n - 1, 1),
        pltpu.roll(jnp.where(lane < 2, other, h), n - 2, 1),
    )


def kernel(
    axis_sizes,
    count_ref,
    rho_ref,
    eps_ref,
    lam_ref,
    vel_ref,
    rows_ref,
    mass_ref,
    cell_ref,
    weak_ref,
    capture_ref,
    binding_ref,
    charge_ref,
    density_out,
    energy_out,
    lepton_out,
    abundance_out,
    xs,
    zs,
    low_in,
    high_in,
    z_in,
    mid,
    weights,
    onehot,
    rate_weak,
    rate_capture,
    start_rows,
    alpha_capture,
    scaled_capture,
    target,
    update,
    deposit,
    send_sem,
    recv_sem,
):
    n_grp, n_brick = axis_sizes
    g = lax.axis_index("grp")
    b = lax.axis_index("brick")
    right = (g, lax.rem(b + 1, n_brick))
    left = (g, lax.rem(b + n_brick - 1, n_brick))
    partner = (lax.rem(g + 1, n_grp), b)
    fields = (rho_ref, eps_ref, lam_ref)
    outs = (density_out, energy_out, lepton_out)
    cx, cy, cz = rho_ref.shape
    capacity, species = rows_ref.shape

    barrier = pltpu.get_barrier_semaphore()
    for neighbour in (left, right, partner):
        pl.semaphore_signal(barrier, inc=1, device_id=neighbour, device_id_type=MESH)

    for f in range(3):
        for p in range(cx):
            xs[0, f, p] = vel_ref[0, p] * fields[f][p]
            zs[0, f, p] = vel_ref[2, p] * fields[f][p]

    pl.semaphore_wait(barrier, 3)

    def copies(stage, f):
        made = []
        for k, (src, dst, device) in enumerate(
            (
                (xs.at[stage, f, pl.ds(0, 2)], high_in.at[stage, f], left),
                (xs.at[stage, f, pl.ds(cx - 2, 2)], low_in.at[stage, f], right),
                (zs.at[stage, f], z_in.at[stage, f], partner),
            )
        ):
            made.append(
                pltpu.make_async_remote_copy(
                    src_ref=src,
                    dst_ref=dst,
                    send_sem=send_sem.at[stage, f, k],
                    recv_sem=recv_sem.at[stage, f, k],
                    device_id=device,
                    device_id_type=MESH,
                )
            )
        return made

    started = [[copies(stage, f) for f in range(3)] for stage in range(2)]
    for f in range(3):
        for copy in started[0][f]:
            copy.start()

    cells = cell_ref[...]
    cell_row = cells // cz
    cell_lane = cells - cell_row * cz
    row_ids = lax.broadcasted_iota(jnp.int32, (cx * cy, capacity), 0)
    onehot[...] = jnp.where(row_ids == cell_row, 1.0, 0.0).astype(bf16)
    lane_ids = lax.broadcasted_iota(jnp.int32, (cz, capacity), 0)
    lane_hit = lane_ids == cell_lane
    picked = []
    for f in range(3):
        high, low = split(fields[f][...].reshape(cx * cy, cz))
        found = dot(high, onehot[...], ((0,), (0,))) + dot(low, onehot[...], ((0,), (0,)))
        picked.append(jnp.sum(jnp.where(lane_hit, found, 0.0), axis=0, keepdims=True))
    rho, eps, lam = picked
    weak_row = 0.62 + 0.04 * rho + 0.05 * (lam / rho)
    capture_row = 0.3 * jax.nn.sigmoid(eps / rho)
    for k in range(capacity // 128):
        part = pl.ds(k * 128, 128)
        cols = slice(k * 128, k * 128 + 128)
        rate_weak[part, :] = jnp.broadcast_to(weak_row[:, cols], (128, 128)).T
        rate_capture[part, :] = jnp.broadcast_to(capture_row[:, cols], (128, 128)).T

    for k, ref in enumerate((weak_ref, capture_ref)):
        high, low = split(ref[...])
        cols = pl.ds(k * species, species)
        weights[0:species, cols] = high
        weights[species : 2 * species, cols] = high
        weights[2 * species : 3 * species, cols] = low

    count = count_ref[0, 0]
    for k in range(capacity // BLOCK):
        part = pl.ds(k * BLOCK, BLOCK)
        row = lax.broadcasted_iota(jnp.int32, (BLOCK, species), 0) + k * BLOCK
        first = jnp.where(row < count, rows_ref[part, :], 0.0)
        start_rows[part, :] = first
        abundance_out[part, :] = first

    def product(values):
        high, low = split(values)
        return dot(jnp.concatenate([high, low, high], axis=1), weights[...])

    def newton_start(turn):
        for k in range(capacity // BLOCK):
            part = pl.ds(k * BLOCK, BLOCK)
            now = abundance_out[part, :]
            made = product(now)
            capture = made[:, species:]
            scaled = rate_capture[part, :]
            alpha = scaled * now[:, 0:1]
            alpha_capture[part, :] = alpha
            scaled_capture[part, :] = scaled * capture
            aim = rate_weak[part, :] * made[:, :species] + alpha * capture
            if turn:
                aim = aim - (now - start_rows[part, :])
            target[part, :] = aim
            update[part, :] = aim

    def sweeps(number):
        def sweep(_, carry):
            for k in range(capacity // BLOCK):
                part = pl.ds(k * BLOCK, BLOCK)
                now = update[part, :]
                made = product(now)
                update[part, :] = target[part, :] + (
                    rate_weak[part, :] * made[:, :species]
                    + alpha_capture[part, :] * made[:, species:]
                    + scaled_capture[part, :] * now[:, 0:1]
                )
            return carry

        lax.fori_loop(0, number, sweep, 0)

    def newton_end():
        for k in range(capacity // BLOCK):
            part = pl.ds(k * BLOCK, BLOCK)
            abundance_out[part, :] = abundance_out[part, :] + update[part, :]

    def tendency(stage, f, field):
        results = []
        line = (
            [low_in[stage, f, 0], low_in[stage, f, 1]]
            + [xs[stage, f, p] for p in range(cx)]
            + [high_in[stage, f, 0], high_in[stage, f, 1]]
        )
        for p in range(cx):
            along_x = five_point(line[p], line[p + 1], line[p + 3], line[p + 4])
            along_y = y_part(vel_ref[1, p] * field[p])
            along_z = z_part(zs[stage, f, p], z_in[stage, f, p])
            results.append((along_x + along_y + along_z) * (-1.0 / 12.0))
        return results

    def half_step(f):
        for copy in started[0][f]:
            copy.wait_recv()
        slopes = tendency(0, f, [fields[f][p] for p in range(cx)])
        for p in range(cx):
            half = fields[f][p] + 0.5 * courant * slopes[p]
            mid[f, p] = half
            xs[1, f, p] = vel_ref[0, p] * half
            zs[1, f, p] = vel_ref[2, p] * half
        for copy in started[1][f]:
            copy.start()

    newton_start(0)
    sweeps(SWEEPS)
    newton_end()
    half_step(0)
    newton_start(1)
    sweeps(SWEEPS // 2)
    half_step(1)
    sweeps(SWEEPS - SWEEPS // 2)
    newton_end()
    half_step(2)

    change_high, change_low = split(abundance_out[...] - start_rows[...])
    table = jnp.concatenate(
        [binding_ref[...], charge_ref[...], jnp.zeros((6, species), f32)], axis=0
    )
    table_high, table_low = split(table)
    gains = (
        dot(table_high, change_high, ((1,), (1,)))
        + dot(table_high, change_low, ((1,), (1,)))
        + dot(table_low, change_high, ((1,), (1,)))
    ) * mass_ref[...]
    for k in range(2):
        placed = jnp.where(lane_hit, gains[k : k + 1, :], 0.0)
        high, low = split(placed)
        deposit[k] = (
            dot(onehot[...], high, ((1,), (1,))) + dot(onehot[...], low, ((1,), (1,)))
        ).reshape(cx, cy, cz)

    for f in range(3):
        for copy in started[1][f]:
            copy.wait_recv()
        slopes = tendency(1, f, [mid[f, p] for p in range(cx)])
        for p in range(cx):
            value = fields[f][p] + courant * slopes[p]
            if f:
                value = value + deposit[f - 1, p]
            outs[f][p] = value

    for stage in range(2):
        for f in range(3):
            for copy in started[stage][f]:
                copy.wait_send()


def settle(a_ref, b_ref, c_ref, d_ref, a_out, b_out, c_out, d_out, sem):
    pairs = ((d_ref, d_out), (a_ref, a_out), (b_ref, b_out), (c_ref, c_out))
    moves = [pltpu.make_async_copy(src, dst, sem.at[k]) for k, (src, dst) in enumerate(pairs)]
    for move in moves:
        move.start()
    for move in moves:
        move.wait()


def on_device(
    axis_sizes,
    density,
    energy_field,
    lepton_field,
    velocity,
    abundance,
    tracer_mass,
    tracer_cell,
    tracer_count,
    weak_rates,
    capture_rates,
    binding,
    charge_ratio,
):
    cx, cy, cz = density.shape
    capacity, species = abundance.shape[2:]
    vmem = pl.BlockSpec(memory_space=pltpu.VMEM)
    field = jax.ShapeDtypeStruct(density.shape, f32)
    rows = pltpu.VMEM((capacity, species), f32)
    advanced = pl.pallas_call(
        functools.partial(kernel, axis_sizes),
        out_shape=(pltpu.VMEM(density.shape, f32),) * 3 + (rows,),
        in_specs=[pl.BlockSpec(memory_space=pltpu.SMEM)] + [vmem] * 11,
        out_specs=(vmem,) * 4,
        scratch_shapes=[
            pltpu.VMEM((2, 3, cx, cy, cz), f32),
            pltpu.VMEM((2, 3, cx, cy, cz), f32),
            pltpu.VMEM((2, 3, 2, cy, cz), f32),
            pltpu.VMEM((2, 3, 2, cy, cz), f32),
            pltpu.VMEM((2, 3, cx, cy, cz), f32),
            pltpu.VMEM((3, cx, cy, cz), f32),
            pltpu.VMEM((3 * species, 2 * species), bf16),
            pltpu.VMEM((cx * cy, capacity), bf16),
            rows,
            rows,
            rows,
            rows,
            rows,
            rows,
            rows,
            pltpu.VMEM((2, cx, cy, cz), f32),
            pltpu.SemaphoreType.DMA((2, 3, 3)),
            pltpu.SemaphoreType.DMA((2, 3, 3)),
        ],
        compiler_params=pltpu.CompilerParams(collective_id=0, has_side_effects=True),
    )(
        tracer_count,
        density,
        energy_field,
        lepton_field,
        velocity,
        abundance.reshape(capacity, species),
        tracer_mass.reshape(1, capacity),
        tracer_cell.reshape(1, capacity),
        weak_rates,
        capture_rates,
        binding.reshape(1, species),
        charge_ratio.reshape(1, species),
    )
    whole = pl.BlockSpec(memory_space=pl.ANY)
    results = pl.pallas_call(
        settle,
        out_shape=(field, field, field, jax.ShapeDtypeStruct((capacity, species), f32)),
        in_specs=[whole] * 4,
        out_specs=(whole,) * 4,
        scratch_shapes=[pltpu.SemaphoreType.DMA((4,))],
    )(*[pltpu.with_memory_space_constraint(a, pltpu.VMEM) for a in advanced])
    return results[0], results[1], results[2], results[3][None, None]


def solution(mesh):
    sizes = (mesh.shape["grp"], mesh.shape["brick"])
    assert sizes[0] == 2
    return jax.shard_map(
        functools.partial(on_device, sizes),
        mesh=mesh,
        in_specs=(
            P("brick", None, "grp"),
            P("brick", None, "grp"),
            P("brick", None, "grp"),
            P(None, "brick", None, "grp"),
            P("grp", "brick", None, None),
            P("grp", "brick", None),
            P("grp", "brick", None),
            P("grp", "brick"),
            P(),
            P(),
            P(),
            P(),
        ),
        out_specs=(
            P("brick", None, "grp"),
            P("brick", None, "grp"),
            P("brick", None, "grp"),
            P("grp", "brick", None, None),
        ),
        check_vma=False,
    )
```

profile of v0, /device:TPU:0, one launch (start us, length us, event | category | flops | bytes accessed | tf_op | source)
XLA Modules:
  0.0 27.3 jit_solution(12680132954511036690)
XLA Ops:
  1.3 25.1 %shard_map.147 = (f32[4,64,128]{2,1,0:T(8,128)S(1)}, f32[4,64,128]{2,1,0:T(8,128)S(1)}, f32[4,64,128]{2,1,0:T(8,128)S(1)}, f32[1024,128]{1,0:T(8,128)S(1)}) custom-call(s32[1,1]{1,0:T(1,128)S(6)} %copy.16.count_ref, f32[4,64,128]{2,1,0:T(8,128)} %rho_ref.1, f32[4,64,128]{2,1,0:T(8,128)} %eps_ref.1, f32[4,64,128]{2,1,0:T(8,128)} %lam_ref.1, ...), custom_call_target="tpu_custom_call" | custom-call | tf_op jit(solution)/shard_map/pallas_call | solution.py:311
  26.4 0.9 %shard_map.148 = (f32[4,64,128]{2,1,0:T(8,128)}, f32[4,64,128]{2,1,0:T(8,128)}, f32[4,64,128]{2,1,0:T(8,128)}, f32[1024,128]{1,0:T(8,128)}) custom-call(f32[4,64,128]{2,1,0:T(8,128)S(1)} %get-tuple-element.12.a_ref, f32[4,64,128]{2,1,0:T(8,128)S(1)} %get-tuple-element.13.b_ref, f32[4,64,128]{2,1,0:T(8,128)S(1)} %get-tuple-element.14.c_ref, ...), custom_call_target="tpu_custom_call" | custom-call | tf_op jit(solution)/shard_map/pallas_call | solution.py:352
where the time goes:
time: 27.5 us; the launch traced here: 27.3 us
  Pallas kernels  26.1 us (95%)
  between operations  1.29 us (5%)
    pallas_call x1, Pallas kernels, on_device(): pl.pallas_call(functools.partial(kernel, axis_sizes), out_shape=(pltpu.VM...  25.1 us
    pallas_call x1, Pallas kernels, on_device(): pl.pallas_call(settle, out_shape=(field, field, field, jax.ShapeDtypeStru...  0.95 us

commit v1 on v0

--- a/solution.py
+++ b/solution.py
@@ -13,6 +13,7 @@
 f32 = jnp.float32
 bf16 = jnp.bfloat16
 BLOCK = 256
+EARLY = 2
 MESH = pl.DeviceIdType.MESH
 
 
@@ -50,27 +51,35 @@
 
 def kernel(
     axis_sizes,
-    count_ref,
-    rho_ref,
-    eps_ref,
-    lam_ref,
-    vel_ref,
-    rows_ref,
-    mass_ref,
-    cell_ref,
-    weak_ref,
-    capture_ref,
-    binding_ref,
-    charge_ref,
+    count_hbm,
+    rho_hbm,
+    eps_hbm,
+    lam_hbm,
+    vel_hbm,
+    rows_hbm,
+    mass_hbm,
+    cell_hbm,
+    weak_hbm,
+    capture_hbm,
+    binding_hbm,
+    charge_hbm,
     density_out,
     energy_out,
     lepton_out,
     abundance_out,
+    count_ref,
+    field,
+    vel,
+    mass_ref,
+    cell_ref,
+    rates,
+    table,
     xs,
     zs,
     low_in,
     high_in,
     z_in,
+    v_in,
     mid,
     weights,
     onehot,
@@ -82,57 +91,136 @@
     target,
     update,
     deposit,
+    load_sem,
     send_sem,
     recv_sem,
+    z_send_sem,
+    z_recv_sem,
+    v_sem,
 ):
     n_grp, n_brick = axis_sizes
     g = lax.axis_index("grp")
     b = lax.axis_index("brick")
+    last = n_brick - 1
     right = (g, lax.rem(b + 1, n_brick))
     left = (g, lax.rem(b + n_brick - 1, n_brick))
     partner = (lax.rem(g + 1, n_grp), b)
-    fields = (rho_ref, eps_ref, lam_ref)
     outs = (density_out, energy_out, lepton_out)
-    cx, cy, cz = rho_ref.shape
-    capacity, species = rows_ref.shape
+    cx, cy, cz = density_out.shape
+    capacity, species = abundance_out.shape
+    assert cx == 4
+    low_pair = pl.ds(0, 2)
+    high_pair = pl.ds(cx - 2, 2)
+    pairs = (low_pair, high_pair)
 
     barrier = pltpu.get_barrier_semaphore()
-    for neighbour in (left, right, partner):
-        pl.semaphore_signal(barrier, inc=1, device_id=neighbour, device_id_type=MESH)
-
-    for f in range(3):
+
+    def greet(device):
+        pl.semaphore_signal(barrier, inc=1, device_id=device, device_id_type=MESH)
+
+    greet(partner)
+
+    @pl.when(b > 0)
+    def _():
+        greet(left)
+
+    @pl.when(b < last)
+    def _():
+        greet(right)
+
+    moves = [
+        pltpu.make_async_copy(src, dst, load_sem.at[k])
+        for k, (src, dst) in enumerate(
+            (
+                (vel_hbm.at[0], vel.at[0]),
+                (rho_hbm, field.at[0]),
+                (eps_hbm, field.at[1]),
+                (lam_hbm, field.at[2]),
+                (vel_hbm.at[2], vel.at[2]),
+                (cell_hbm, cell_ref),
+                (vel_hbm.at[1], vel.at[1]),
+                (weak_hbm, rates.at[0]),
+                (capture_hbm, rates.at[1]),
+                (count_hbm, count_ref),
+                (rows_hbm, start_rows),
+                (mass_hbm, mass_ref),
+                (binding_hbm, table.at[pl.ds(0, 1)]),
+                (charge_hbm, table.at[pl.ds(1, 1)]),
+            )
+        )
+    ]
+    for move in moves:
+        move.start()
+
+    def x_copy(stage, f, side):
+        src, dst, device = (
+            (xs.at[stage, f, low_pair], high_in.at[stage, f], left),
+            (xs.at[stage, f, high_pair], low_in.at[stage, f], right),
+        )[side]
+        return pltpu.make_async_remote_copy(
+            src_ref=src,
+            dst_ref=dst,
+            send_sem=send_sem.at[stage, f, side],
+            recv_sem=recv_sem.at[stage, f, side],
+            device_id=device,
+            device_id_type=MESH,
+        )
+
+    def z_copy(stage, f, side):
+        return pltpu.make_async_remote_copy(
+            src_ref=zs.at[stage, f, pairs[side]],
+            dst_ref=z_in.at[stage, f, pairs[side]],
+            send_sem=z_send_sem.at[stage, f, side],
+            recv_sem=z_recv_sem.at[stage, f, side],
+            device_id=partner,
+            device_id_type=MESH,
+        )
+
+    def v_copy():
+        return pltpu.make_async_remote_copy(
+            src_ref=vel.at[0, high_pair],
+            dst_ref=v_in,
+            send_sem=v_sem.at[0],
+            recv_sem=v_sem.at[1],
+            device_id=right,
+            device_id_type=MESH,
+        )
+
+    moves[0].wait()
+    for f in range(3):
+        moves[1 + f].wait()
         for p in range(cx):
-            xs[0, f, p] = vel_ref[0, p] * fields[f][p]
-            zs[0, f, p] = vel_ref[2, p] * fields[f][p]
-
-    pl.semaphore_wait(barrier, 3)
-
-    def copies(stage, f):
-        made = []
-        for k, (src, dst, device) in enumerate(
-            (
-                (xs.at[stage, f, pl.ds(0, 2)], high_in.at[stage, f], left),
-                (xs.at[stage, f, pl.ds(cx - 2, 2)], low_in.at[stage, f], right),
-                (zs.at[stage, f], z_in.at[stage, f], partner),
-            )
-        ):
-            made.append(
-                pltpu.make_async_remote_copy(
-                    src_ref=src,
-                    dst_ref=dst,
-                    send_sem=send_sem.at[stage, f, k],
-                    recv_sem=recv_sem.at[stage, f, k],
-                    device_id=device,
-                    device_id_type=MESH,
-                )
-            )
-        return made
-
-    started = [[copies(stage, f) for f in range(3)] for stage in range(2)]
-    for f in range(3):
-        for copy in started[0][f]:
-            copy.start()
-
+            xs[0, f, p] = vel[0, p] * field[f, p]
+
+    @pl.when(b == 0)
+    def _():
+        pl.semaphore_wait(barrier, 2)
+        greet(left)
+
+    @pl.when(b > 0)
+    def _():
+        pl.semaphore_wait(barrier, 3)
+
+    @pl.when(b == last)
+    def _():
+        greet(right)
+
+    for f in range(3):
+        x_copy(0, f, 1).start()
+
+        @pl.when(b > 0)
+        def _():
+            x_copy(0, f, 0).start()
+
+    moves[4].wait()
+    for f in range(3):
+        for p in range(cx):
+            zs[0, f, p] = vel[2, p] * field[f, p]
+        for side in range(2):
+            z_copy(0, f, side).start()
+
+    for move in moves[5:]:
+        move.wait()
     cells = cell_ref[...]
     cell_row = cells // cz
     cell_lane = cells - cell_row * cz
@@ -142,7 +230,7 @@
     lane_hit = lane_ids == cell_lane
     picked = []
     for f in range(3):
-        high, low = split(fields[f][...].reshape(cx * cy, cz))
+        high, low = split(field[f].reshape(cx * cy, cz))
         found = dot(high, onehot[...], ((0,), (0,))) + dot(low, onehot[...], ((0,), (0,)))
         picked.append(jnp.sum(jnp.where(lane_hit, found, 0.0), axis=0, keepdims=True))
     rho, eps, lam = picked
@@ -154,18 +242,18 @@
         rate_weak[part, :] = jnp.broadcast_to(weak_row[:, cols], (128, 128)).T
         rate_capture[part, :] = jnp.broadcast_to(capture_row[:, cols], (128, 128)).T
 
-    for k, ref in enumerate((weak_ref, capture_ref)):
-        high, low = split(ref[...])
+    for k in range(2):
+        high, low = split(rates[k])
         cols = pl.ds(k * species, species)
         weights[0:species, cols] = high
         weights[species : 2 * species, cols] = high
         weights[2 * species : 3 * species, cols] = low
 
-    count = count_ref[0, 0]
+    count = count_ref[...]
     for k in range(capacity // BLOCK):
         part = pl.ds(k * BLOCK, BLOCK)
         row = lax.broadcasted_iota(jnp.int32, (BLOCK, species), 0) + k * BLOCK
-        first = jnp.where(row < count, rows_ref[part, :], 0.0)
+        first = jnp.where(row < count, start_rows[part, :], 0.0)
         start_rows[part, :] = first
         abundance_out[part, :] = first
 
@@ -209,74 +297,152 @@
             part = pl.ds(k * BLOCK, BLOCK)
             abundance_out[part, :] = abundance_out[part, :] + update[part, :]
 
-    def tendency(stage, f, field):
+    half = 0.5 * courant / 12.0
+    full = courant / 12.0
+
+    def inside(stage, f, quantity, flux):
         results = []
-        line = (
-            [low_in[stage, f, 0], low_in[stage, f, 1]]
-            + [xs[stage, f, p] for p in range(cx)]
-            + [high_in[stage, f, 0], high_in[stage, f, 1]]
-        )
         for p in range(cx):
-            along_x = five_point(line[p], line[p + 1], line[p + 3], line[p + 4])
-            along_y = y_part(vel_ref[1, p] * field[p])
-            along_z = z_part(zs[stage, f, p], z_in[stage, f, p])
-            results.append((along_x + along_y + along_z) * (-1.0 / 12.0))
+            total = y_part(vel[1, p] * quantity[p]) + z_part(zs[stage, f, p], z_in[stage, f, p])
+            for step, factor in ((1, 8.0), (-1, -8.0), (2, -1.0), (-2, 1.0)):
+                if 0 <= p + step < cx:
+                    total = total + factor * flux[p + step]
+            results.append(total)
         return results
 
-    def half_step(f):
-        for copy in started[0][f]:
-            copy.wait_recv()
-        slopes = tendency(0, f, [fields[f][p] for p in range(cx)])
+    def from_low(stage, f):
+        near, far = low_in[stage, f, 1], low_in[stage, f, 0]
+        return far - 8.0 * near, near
+
+    def from_high(stage, f):
+        near, far = high_in[stage, f, 0], high_in[stage, f, 1]
+        return -near, 8.0 * near - far
+
+    def half_inside(f):
+        for side in range(2):
+            z_copy(0, f, side).wait_recv()
+        slopes = inside(0, f, [field[f, p] for p in range(cx)], [xs[0, f, p] for p in range(cx)])
         for p in range(cx):
-            half = fields[f][p] + 0.5 * courant * slopes[p]
-            mid[f, p] = half
-            xs[1, f, p] = vel_ref[0, p] * half
-            zs[1, f, p] = vel_ref[2, p] * half
-        for copy in started[1][f]:
-            copy.start()
+            mid[f, p] = field[f, p] - half * slopes[p]
+
+    def send_flux(f, side):
+        for p in (0, 1) if side == 0 else (cx - 2, cx - 1):
+            xs[1, f, p] = vel[0, p] * mid[f, p]
+        x_copy(1, f, side).start()
+
+    def finish_half(f, side, send=True):
+        x_copy(0, f, 1 - side).wait_recv()
+        extra = from_low(0, f) if side == 0 else from_high(0, f)
+        for p, part in zip((0, 1) if side == 0 else (cx - 2, cx - 1), extra):
+            value = mid[f, p] - half * part
+            mid[f, p] = value
+            if send:
+                xs[1, f, p] = vel[0, p] * value
+            zs[1, f, p] = vel[2, p] * value
+        if send:
+            x_copy(1, f, side).start()
+        z_copy(1, f, side).start()
+
+    def finish_half_sides(f):
+        @pl.when(b < last)
+        def _():
+            finish_half(f, 1)
+
+        @pl.when(b > 0)
+        def _():
+            finish_half(f, 0)
 
     newton_start(0)
-    sweeps(SWEEPS)
+    sweeps(EARLY)
+    for f in range(3):
+        half_inside(f)
+
+    @pl.when(b == last)
+    def _():
+        for f in range(3):
+            send_flux(f, 1)
+        v_copy().start()
+
+    finish_half_sides(0)
+    sweeps(SWEEPS - EARLY)
     newton_end()
-    half_step(0)
     newton_start(1)
+
+    @pl.when(b == 0)
+    def _():
+        pl.semaphore_wait(barrier, 1)
+        for f in range(3):
+            x_copy(0, f, 0).start()
+
+    finish_half_sides(1)
     sweeps(SWEEPS // 2)
-    half_step(1)
+    finish_half_sides(2)
     sweeps(SWEEPS - SWEEPS // 2)
     newton_end()
-    half_step(2)
 
     change_high, change_low = split(abundance_out[...] - start_rows[...])
-    table = jnp.concatenate(
-        [binding_ref[...], charge_ref[...], jnp.zeros((6, species), f32)], axis=0
-    )
-    table_high, table_low = split(table)
+    pair = jnp.concatenate([table[...], jnp.zeros((6, species), f32)], axis=0)
+    table_high, table_low = split(pair)
     gains = (
         dot(table_high, change_high, ((1,), (1,)))
         + dot(table_high, change_low, ((1,), (1,)))
         + dot(table_low, change_high, ((1,), (1,)))
     ) * mass_ref[...]
     for k in range(2):
-        placed = jnp.where(lane_hit, gains[k : k + 1, :], 0.0)
+        placed = jnp.where(lane_ids == cell_lane, gains[k : k + 1, :], 0.0)
         high, low = split(placed)
         deposit[k] = (
             dot(onehot[...], high, ((1,), (1,))) + dot(onehot[...], low, ((1,), (1,)))
         ).reshape(cx, cy, cz)
 
-    for f in range(3):
-        for copy in started[1][f]:
-            copy.wait_recv()
-        slopes = tendency(1, f, [mid[f, p] for p in range(cx)])
+    @pl.when(b == 0)
+    def _():
+        for f in range(3):
+            finish_half(f, 0)
+
+    @pl.when(b == last)
+    def _():
+        for f in range(3):
+            finish_half(f, 1, send=False)
+
+    for f in range(3):
+        for side in range(2):
+            z_copy(1, f, side).wait_recv()
+        slopes = inside(
+            1, f, [mid[f, p] for p in range(cx)], [vel[0, p] * mid[f, p] for p in range(cx)]
+        )
         for p in range(cx):
-            value = fields[f][p] + courant * slopes[p]
+            value = field[f, p] - full * slopes[p]
             if f:
                 value = value + deposit[f - 1, p]
             outs[f][p] = value
 
+    @pl.when(b == 0)
+    def _():
+        v_copy().wait_recv()
+
+    for f in range(3):
+        for side in range(2):
+            x_copy(1, f, side).wait_recv()
+
+        @pl.when(b == 0)
+        def _():
+            share = (-xs[0, f, 0], 8.0 * xs[0, f, 0] - xs[0, f, 1])
+            for p in range(2):
+                low_in[1, f, p] = low_in[1, f, p] - half * v_in[p] * share[p]
+
+        for p, part in enumerate(from_low(1, f) + from_high(1, f)):
+            outs[f][p] = outs[f][p] - full * part
+
     for stage in range(2):
         for f in range(3):
-            for copy in started[stage][f]:
-                copy.wait_send()
+            for side in range(2):
+                x_copy(stage, f, side).wait_send()
+                z_copy(stage, f, side).wait_send()
+
+    @pl.when(b == last)
+    def _():
+        v_copy().wait_send()
 
 
 def settle(a_ref, b_ref, c_ref, d_ref, a_out, b_out, c_out, d_out, sem):
@@ -311,14 +477,22 @@
     advanced = pl.pallas_call(
         functools.partial(kernel, axis_sizes),
         out_shape=(pltpu.VMEM(density.shape, f32),) * 3 + (rows,),
-        in_specs=[pl.BlockSpec(memory_space=pltpu.SMEM)] + [vmem] * 11,
+        in_specs=[pl.BlockSpec(memory_space=pl.ANY)] * 12,
         out_specs=(vmem,) * 4,
         scratch_shapes=[
+            pltpu.VMEM((1, 1), jnp.int32),
+            pltpu.VMEM((3, cx, cy, cz), f32),
+            pltpu.VMEM((3, cx, cy, cz), f32),
+            pltpu.VMEM((1, capacity), f32),
+            pltpu.VMEM((1, capacity), jnp.int32),
+            pltpu.VMEM((2, species, species), f32),
+            pltpu.VMEM((2, species), f32),
             pltpu.VMEM((2, 3, cx, cy, cz), f32),
             pltpu.VMEM((2, 3, cx, cy, cz), f32),
             pltpu.VMEM((2, 3, 2, cy, cz), f32),
             pltpu.VMEM((2, 3, 2, cy, cz), f32),
             pltpu.VMEM((2, 3, cx, cy, cz), f32),
+            pltpu.VMEM((2, cy, cz), f32),
             pltpu.VMEM((3, cx, cy, cz), f32),
             pltpu.VMEM((3 * species, 2 * species), bf16),
             pltpu.VMEM((cx * cy, capacity), bf16),
@@ -330,8 +504,12 @@
             rows,
             rows,
             pltpu.VMEM((2, cx, cy, cz), f32),
-            pltpu.SemaphoreType.DMA((2, 3, 3)),
-            pltpu.SemaphoreType.DMA((2, 3, 3)),
+            pltpu.SemaphoreType.DMA((14,)),
+            pltpu.SemaphoreType.DMA((2, 3, 2)),
+            pltpu.SemaphoreType.DMA((2, 3, 2)),
+            pltpu.SemaphoreType.DMA((2, 3, 2)),
+            pltpu.SemaphoreType.DMA((2, 3, 2)),
+            pltpu.SemaphoreType.DMA((2,)),
         ],
         compiler_params=pltpu.CompilerParams(collective_id=0, has_side_effects=True),
     )(

time: 27.5 us -> 26.5 us (0.964)
  the two profiles are of different devices: /device:TPU:0 before, /device:TPU:2 now
where the time goes in v1:
time: 26.5 us; the launch traced here: 26.4 us
  Pallas kernels  25.1 us (95%)
  between operations  1.29 us (5%)
    pallas_call x1, Pallas kernels, on_device(): pl.pallas_call(functools.partial(kernel, axis_sizes), out_shape=(pltpu.VM...  24.1 us
    pallas_call x1, Pallas kernels, on_device(): pl.pallas_call(settle, out_shape=(field, field, field, jax.ShapeDtypeStru...  0.95 us

profile of v1, /device:TPU:2, one launch (start us, length us, event | category | flops | bytes accessed | tf_op | source)
XLA Modules:
  0.0 26.4 jit_solution(16006038365189154072)
XLA Ops:
  1.3 24.1 %shard_map.147 = (f32[4,64,128]{2,1,0:T(8,128)S(1)}, f32[4,64,128]{2,1,0:T(8,128)S(1)}, f32[4,64,128]{2,1,0:T(8,128)S(1)}, f32[1024,128]{1,0:T(8,128)S(1)}) custom-call(s32[1,1]{1,0:T(1,128)S(6)} %copy.16.count_hbm, f32[4,64,128]{2,1,0:T(8,128)} %rho_hbm.1, f32[4,64,128]{2,1,0:T(8,128)} %eps_hbm.1, f32[4,64,128]{2,1,0:T(8,128)} %lam_hbm.1, ...), custom_call_target="tpu_custom_call" | custom-call | tf_op jit(solution)/shard_map/pallas_call | solution.py:477
  25.4 0.9 %shard_map.148 = (f32[4,64,128]{2,1,0:T(8,128)}, f32[4,64,128]{2,1,0:T(8,128)}, f32[4,64,128]{2,1,0:T(8,128)}, f32[1024,128]{1,0:T(8,128)}) custom-call(f32[4,64,128]{2,1,0:T(8,128)S(1)} %get-tuple-element.12.a_ref, f32[4,64,128]{2,1,0:T(8,128)S(1)} %get-tuple-element.13.b_ref, f32[4,64,128]{2,1,0:T(8,128)S(1)} %get-tuple-element.14.c_ref, ...), custom_call_target="tpu_custom_call" | custom-call | tf_op jit(solution)/shard_map/pallas_call | solution.py:530

commit v2 on v1

--- a/solution.py
+++ b/solution.py
@@ -13,7 +13,7 @@
 f32 = jnp.float32
 bf16 = jnp.bfloat16
 BLOCK = 256
-EARLY = 2
+ROW = 4
 MESH = pl.DeviceIdType.MESH
 
 
@@ -102,6 +102,7 @@
     g = lax.axis_index("grp")
     b = lax.axis_index("brick")
     last = n_brick - 1
+    spot = lax.rem(b, ROW)
     right = (g, lax.rem(b + 1, n_brick))
     left = (g, lax.rem(b + n_brick - 1, n_brick))
     partner = (lax.rem(g + 1, n_grp), b)
@@ -205,12 +206,50 @@
     def _():
         greet(right)
 
-    for f in range(3):
-        x_copy(0, f, 1).start()
-
-        @pl.when(b > 0)
+    def at(*spots):
+        found = spot == spots[0]
+        for other in spots[1:]:
+            found = jnp.logical_or(found, spot == other)
+        return found
+
+    far_left = jnp.logical_and(spot == 0, b > 0)
+    far_right = jnp.logical_and(spot == ROW - 1, b < last)
+
+    def send_near(f):
+        @pl.when(at(0, 1))
+        def _():
+            x_copy(0, f, 1).start()
+
+        @pl.when(at(1, 2))
         def _():
             x_copy(0, f, 0).start()
+
+        @pl.when(at(3))
+        def _():
+            x_copy(0, f, 0).start()
+
+        @pl.when(at(2))
+        def _():
+            x_copy(0, f, 1).start()
+
+    def send_far(f):
+        @pl.when(far_left)
+        def _():
+            x_copy(0, f, 0).start()
+
+        @pl.when(far_right)
+        def _():
+            x_copy(0, f, 1).start()
+
+    def send_seam(f):
+        @pl.when(b == last)
+        def _():
+            x_copy(0, f, 1).start()
+
+    send_near(0)
+
+    send_far(0)
+    send_seam(0)
 
     moves[4].wait()
     for f in range(3):
@@ -343,42 +382,89 @@
             x_copy(1, f, side).start()
         z_copy(1, f, side).start()
 
-    def finish_half_sides(f):
-        @pl.when(b < last)
+    held_up = b == ROW - 2
+
+    def finish_near(f):
+        @pl.when(at(1, 2, 3) if f == 2 else at(2, 3))
+        def _():
+            finish_half(f, 0)
+
+        @pl.when(jnp.logical_and(at(0, 1, 2), jnp.logical_not(held_up)) if f else at(0, 1, 2))
         def _():
             finish_half(f, 1)
 
-        @pl.when(b > 0)
+        if f < 2:
+
+            @pl.when(at(1))
+            def _():
+                finish_half(f, 0)
+
+    def finish_held_up(f):
+        @pl.when(held_up)
+        def _():
+            finish_half(f, 1)
+
+    def finish_far(f):
+        @pl.when(far_left)
         def _():
             finish_half(f, 0)
 
+        @pl.when(far_right)
+        def _():
+            finish_half(f, 1)
+
+    def seam_flux(f):
+        @pl.when(b == last)
+        def _():
+            send_flux(f, 1)
+            if f == 0:
+                v_copy().start()
+
+    def seam_back(f):
+        @pl.when(b == 0)
+        def _():
+            if f == 0:
+                pl.semaphore_wait(barrier, 1)
+            x_copy(0, f, 0).start()
+
+    def seam_half(f):
+        @pl.when(b == 0)
+        def _():
+            finish_half(f, 0)
+
+    send_near(1)
+    send_seam(1)
     newton_start(0)
-    sweeps(EARLY)
+    sweeps(2)
+    send_far(1)
+    send_seam(2)
     for f in range(3):
         half_inside(f)
-
-    @pl.when(b == last)
-    def _():
-        for f in range(3):
-            send_flux(f, 1)
-        v_copy().start()
-
-    finish_half_sides(0)
-    sweeps(SWEEPS - EARLY)
+    send_near(2)
+    seam_back(0)
+    finish_near(0)
+    sweeps(3)
+    send_far(2)
+    seam_flux(0)
+    seam_back(1)
+    sweeps(SWEEPS - 5)
     newton_end()
     newton_start(1)
-
-    @pl.when(b == 0)
-    def _():
-        pl.semaphore_wait(barrier, 1)
-        for f in range(3):
-            x_copy(0, f, 0).start()
-
-    finish_half_sides(1)
+    finish_near(1)
+    finish_far(0)
+    seam_flux(1)
+    seam_flux(2)
+    seam_back(2)
     sweeps(SWEEPS // 2)
-    finish_half_sides(2)
-    sweeps(SWEEPS - SWEEPS // 2)
+    finish_near(2)
+    seam_half(0)
+    sweeps(2)
+    finish_far(1)
+    finish_held_up(1)
+    seam_half(1)
+    sweeps(SWEEPS - SWEEPS // 2 - 2)
     newton_end()
+    seam_half(2)
 
     change_high, change_low = split(abundance_out[...] - start_rows[...])
     pair = jnp.concatenate([table[...], jnp.zeros((6, species), f32)], axis=0)
@@ -395,10 +481,8 @@
             dot(onehot[...], high, ((1,), (1,))) + dot(onehot[...], low, ((1,), (1,)))
         ).reshape(cx, cy, cz)
 
-    @pl.when(b == 0)
-    def _():
-        for f in range(3):
-            finish_half(f, 0)
+    finish_far(2)
+    finish_held_up(2)
 
     @pl.when(b == last)
     def _():

time: 26.5 us -> 25.2 us (0.951)
  the two profiles are of different devices: /device:TPU:2 before, /device:TPU:4 now
where the time goes in v2:
time: 25.2 us; the launch traced here: 25 us
  Pallas kernels  23.7 us (94%)
  between operations  1.29 us (5%)
    pallas_call x1, Pallas kernels, on_device(): pl.pallas_call(functools.partial(kernel, axis_sizes), out_shape=(pltpu.VM...  22.8 us
    pallas_call x1, Pallas kernels, on_device(): pl.pallas_call(settle, out_shape=(field, field, field, jax.ShapeDtypeStru...  0.95 us

profile of v2, /device:TPU:4, one launch (start us, length us, event | category | flops | bytes accessed | tf_op | source)
XLA Modules:
  0.0 25.0 jit_solution(6918748352679977519)
XLA Ops:
  1.3 22.8 %shard_map.147 = (f32[4,64,128]{2,1,0:T(8,128)S(1)}, f32[4,64,128]{2,1,0:T(8,128)S(1)}, f32[4,64,128]{2,1,0:T(8,128)S(1)}, f32[1024,128]{1,0:T(8,128)S(1)}) custom-call(s32[1,1]{1,0:T(1,128)S(6)} %copy.16.count_hbm, f32[4,64,128]{2,1,0:T(8,128)} %rho_hbm.1, f32[4,64,128]{2,1,0:T(8,128)} %eps_hbm.1, f32[4,64,128]{2,1,0:T(8,128)} %lam_hbm.1, ...), custom_call_target="tpu_custom_call" | custom-call | tf_op jit(solution)/shard_map/pallas_call | solution.py:561
  24.0 0.9 %shard_map.148 = (f32[4,64,128]{2,1,0:T(8,128)}, f32[4,64,128]{2,1,0:T(8,128)}, f32[4,64,128]{2,1,0:T(8,128)}, f32[1024,128]{1,0:T(8,128)}) custom-call(f32[4,64,128]{2,1,0:T(8,128)S(1)} %get-tuple-element.12.a_ref, f32[4,64,128]{2,1,0:T(8,128)S(1)} %get-tuple-element.13.b_ref, f32[4,64,128]{2,1,0:T(8,128)S(1)} %get-tuple-element.14.c_ref, ...), custom_call_target="tpu_custom_call" | custom-call | tf_op jit(solution)/shard_map/pallas_call | solution.py:614
